TPU v7x, 256 devices: a whole 4x4x8 slice. The times are simulated.
256 devices in a mesh: row: 8 (over z), col: 32 (over y, x, core).
Axes of the slice: x: 4, y: 4, z: 8, core: 2. Of those that a mesh axis runs over, the one named last changes fastest.
Arguments:
- amps: bfloat16 [384, 131072], P('row', 'col'), may hold values from -6 to 6
- integrals: bfloat16 [131072, 8192], P('col', 'row'), may hold values from -0.046875 to 0.046875
- cd_first: int32 [131072], P('col'), may hold values from 0 to 2399
- cd_second: int32 [131072], P('col'), may hold values from 0 to 2399
- ab_first: int32 [8192], P('row'), may hold values from 0 to 2399
- ab_second: int32 [8192], P('row'), may hold values from 0 to 2399
- occ_first: int32 [384], P('col'), may hold values from 0 to 199
- occ_second: int32 [384], P('col'), may hold values from 0 to 199
- virt_irrep: int32 [2400], replicated, may hold values from 0 to 7
- occ_energy: float32 [200], replicated, may hold values from -2 to -0.5
- virt_energy: float32 [2400], replicated, may hold values from 0.2 to 3
Outputs:
- update: float32 [384, 8192], P('col', 'row')
All inputs are finite; a program needn't handle non-finite values.
Results may differ from a plain program's by a relative error of at most 0.0003.
Values may be sent and summed in bfloat16 or wider, within the bound.
No kernel may reach another device: no remote copies, remote signals or barrier semaphores. Data moves between devices by JAX's collectives and lax.ppermute only.
A program may use at most 64 MiB of HBM per device.

v0:
```python
import jax
import jax.numpy as jnp
from jax import lax
from jax.sharding import PartitionSpec as P


def table_lookup(values_table, positions):
    row_width = 64
    row_count = -(-values_table.shape[0] // row_width)
    padded_table = jnp.pad(
        values_table, (0, row_count * row_width - values_table.shape[0])
    ).reshape(row_count, row_width)
    high_hot = (
        (positions // row_width)[:, None] == jnp.arange(row_count, dtype=jnp.int32)[None, :]
    ).astype(jnp.float32)
    low_hot = (
        (positions % row_width)[:, None] == jnp.arange(row_width, dtype=jnp.int32)[None, :]
    ).astype(jnp.float32)
    picked = jnp.dot(
        high_hot, padded_table, precision=lax.Precision.HIGHEST, preferred_element_type=jnp.float32
    )
    return jnp.sum(picked * low_hot, axis=1)


def irrep_of(labels_float, first_orb, second_orb):
    first_label = table_lookup(labels_float, first_orb).astype(jnp.int32)
    second_label = table_lookup(labels_float, second_orb).astype(jnp.int32)
    return jnp.bitwise_xor(first_label, second_label)


def on_device(
    amps,
    integrals,
    cd_first,
    cd_second,
    ab_first,
    ab_second,
    occ_first,
    occ_second,
    virt_irrep,
    occ_energy,
    virt_energy,
):
    labels_float = virt_irrep.astype(jnp.float32)
    irrep_cd = irrep_of(labels_float, cd_first, cd_second)
    irrep_ab = irrep_of(labels_float, ab_first, ab_second)
    masked = jnp.where(irrep_cd[:, None] == irrep_ab[None, :], integrals, jnp.zeros_like(integrals))
    partial_sums = jnp.dot(
        lax.all_gather(amps, "row", axis=0, tiled=True), masked, preferred_element_type=jnp.float32
    )
    own_rows = occ_first.shape[0]
    summed = lax.psum(partial_sums, "col")
    ladder = lax.dynamic_slice_in_dim(summed, lax.axis_index("col") * own_rows, own_rows, 0)
    virt_part = table_lookup(virt_energy, ab_first) + table_lookup(virt_energy, ab_second)
    occ_part = table_lookup(occ_energy, occ_first) + table_lookup(occ_energy, occ_second)
    denom = virt_part[None, :] - occ_part[:, None]
    return ladder / denom


def solution(mesh):
    in_specs = (
        P("row", "col"),
        P("col", "row"),
        P("col"),
        P("col"),
        P("row"),
        P("row"),
        P("col"),
        P("col"),
        P(),
        P(),
        P(),
    )
    out_specs = P("col", "row")
    return jax.shard_map(
        on_device, mesh=mesh, in_specs=in_specs, out_specs=out_specs, check_vma=False
    )
```

profile of v0, /device:TPU:6, one launch (start us, length us, event | category | flops | bytes accessed | tf_op | source)
XLA Modules:
  0.0 190.4 jit_solution(7204045527473177920)
XLA Ops:
  6.5 0.0 all-gather.2.cloned.1.call-start
  6.5 0.7 all-gather.2.cloned.1.call-update
  7.3 0.0 all-reduce.5.cloned.1.call-start
  7.3 0.7 convert_element_type.57
  8.0 0.1 reshape.50
  8.1 0.7 add_select_fusion.5
  8.8 0.6 fusion.8
  9.4 0.7 add_select_fusion.7
  10.1 0.6 fusion.7
  10.7 0.7 add_select_fusion.2
  11.4 0.7 fusion.5
  12.1 0.7 add_select_fusion
  12.8 0.7 fusion.6
  13.5 0.0 copy-start.2
  13.6 0.0 copy-start.1
  13.6 0.0 copy-start
  13.6 0.0 copy-start.3
  13.6 43.5 %all-gather.2.cloned.1.call-done = bf16[384,4096]{1,0:T(8,128)(2,1)} async-done(((bf16[48,4096]{1,0:T(8,128)(2,1)}), bf16[384,4096]{1,0:T(8,128)(2,1)}) %all-gather.2.cloned.1.call-update) | async-done | bytes 3145744 | tf_op jit(solution)/shard_map/all_gather | solution.py:49
  57.1 9.0 %fusion.4 = f32[384,1024]{1,0:T(8,128)} fusion(bf16[384,4096]{1,0:T(8,128)(2,1)} %all-gather.2.cloned.1.call-done, bf16[4096,1024]{1,0:T(8,128)(2,1)} %param.12, s32[1024]{0:T(1024)S(1)} %convert_xor_fusion.1, s32[4096]{0:T(1024)S(1)} %convert_xor_fusion), kind=kOutput, calls=%fused_computation.7 | convolution fusion | flops 3229614080 | bytes 13127680 | tf_op jit(solution)/shard_map/dot_general | solution.py:48
  66.1 0.0 all-reduce.5.cloned.1.call-update
  66.1 0.0 copy-done.2
  66.1 0.0 copy-done.1
  66.2 0.1 reshape.52
  66.2 0.0 copy-done
  66.2 0.1 reshape.51
  66.3 0.3 fusion.11
  66.6 0.0 copy-done.3
  66.6 0.3 fusion.12
  67.0 0.6 fusion.10
  67.5 0.6 fusion.9
  68.1 113.8 %all-reduce.5.cloned.1.call-done = f32[384,1024]{1,0:T(8,128)} async-done(((f32[384,1024]{1,0:T(8,128)}), f32[384,1024]{1,0:T(8,128)}) %all-reduce.5.cloned.1.call-update) | async-done | bytes 1572880 | tf_op jit(solution)/shard_map/psum | solution.py:52
  181.9 1.6 subtract_divide_fusion
  (9 shorter events, 0.1 us)
Async XLA Ops:
  6.5 50.5 %all-gather.2.cloned.1.call-start = ((), (), s32[]{:S(2)}) async-start(), calls=%async_computation | async-start | bytes 3538944 | tf_op jit(solution)/shard_map/all_gather | solution.py:49
  7.3 174.7 %all-reduce.5.cloned.1.call-start = ((), (), s32[]{:S(2)}) async-start(), calls=%async_computation.1 | async-start | bytes 3145728 | tf_op jit(solution)/shard_map/psum | solution.py:52
  13.5 52.5 %copy-start.2 = (s32[12]{0:T(128)S(1)}, s32[12]{0:T(128)}, u32[]{:S(2)}) copy-start(s32[12]{0:T(128)} %param.17) | copy-start | bytes 148
  13.6 52.6 %copy-start.1 = (f32[200]{0:T(256)S(1)}, f32[200]{0:T(256)}, u32[]{:S(2)}) copy-start(f32[200]{0:T(256)} %param.20) | copy-start | bytes 2404
  13.6 52.7 %copy-start = (f32[2400]{0:T(1024)S(1)}, f32[2400]{0:T(1024)}, u32[]{:S(2)}) copy-start(f32[2400]{0:T(1024)} %param.21) | copy-start | bytes 28804
  13.6 53.0 %copy-start.3 = (s32[12]{0:T(128)S(1)}, s32[12]{0:T(128)}, u32[]{:S(2)}) copy-start(s32[12]{0:T(128)} %param.18) | copy-start | bytes 148
Sparse Core Ops, SparseCore 0:
  9.1 47.8 all-gather.1
  66.2 115.6 all-reduce.4
where the time goes:
time: 191 us; the launch traced here: 190 us
  waiting for transfers between devices  158 us (83%)
  between operations  13.5 us (7%)
  matrix products  13.3 us (7%)
  other arithmetic  5.24 us (3%)
    psum x1, waiting for transfers between devices, on_device(): summed = lax.psum(partial_sums, 'col')  114 us
    all_gather x1, waiting for transfers between devices, on_device(): lax.all_gather(amps, 'row', axis=0, tiled=True)  43.5 us
    dot_general x1, matrix products, on_device(): jnp.dot(lax.all_gather(amps, 'row', axis=0, tiled=True), masked, preferre...  9 us
    dot_general x8, matrix products, table_lookup(): jnp.dot(high_hot, padded_table, precision=lax.Precision.HIGHEST, preferre...  4.28 us
  transfers between devices with their start and end apart: 2, of which 2 were waited for; matrix products, arithmetic and copies ran while one was open for 4% of the time, Pallas kernels for 0%

commit v1 on v0

--- a/solution.py
+++ b/solution.py
@@ -2,6 +2,27 @@
 import jax.numpy as jnp
 from jax import lax
 from jax.sharding import PartitionSpec as P
+
+
+def collect(x, axis, dim):
+    size, place, span = (lax.axis_size(axis), lax.axis_index(axis), x.shape[dim])
+    right = [(i, (i + 1) % size) for i in range(size)]
+    left = [(i, (i - 1) % size) for i in range(size)]
+    out = jnp.zeros((*x.shape[:dim], size * span, *x.shape[dim + 1 :]), x.dtype)
+    out = lax.dynamic_update_slice_in_dim(out, x, place * span, axis=dim)
+    from_left = from_right = x
+    half = size // 2
+    for turn in range(1, half + 1):
+        from_left = lax.ppermute(from_left, axis, right)
+        out = lax.dynamic_update_slice_in_dim(
+            out, from_left, (place - turn) % size * span, axis=dim
+        )
+        if turn < size - half:
+            from_right = lax.ppermute(from_right, axis, left)
+            out = lax.dynamic_update_slice_in_dim(
+                out, from_right, (place + turn) % size * span, axis=dim
+            )
+    return out
 
 
 def table_lookup(values_table, positions):
@@ -45,9 +66,7 @@
     irrep_cd = irrep_of(labels_float, cd_first, cd_second)
     irrep_ab = irrep_of(labels_float, ab_first, ab_second)
     masked = jnp.where(irrep_cd[:, None] == irrep_ab[None, :], integrals, jnp.zeros_like(integrals))
-    partial_sums = jnp.dot(
-        lax.all_gather(amps, "row", axis=0, tiled=True), masked, preferred_element_type=jnp.float32
-    )
+    partial_sums = jnp.dot(collect(amps, "row", 0), masked, preferred_element_type=jnp.float32)
     own_rows = occ_first.shape[0]
     summed = lax.psum(partial_sums, "col")
     ladder = lax.dynamic_slice_in_dim(summed, lax.axis_index("col") * own_rows, own_rows, 0)

time: 191 us -> 183 us (0.958)
  waiting for transfers between devices: 158 us -> 143 us
  starting transfers between devices: 0.04 us -> 12.3 us
  matrix products: 13.3 us -> 9.04 us
    all_gather x1 -> x0, waiting for transfers between devices: 43.5 us -> none  [on_device(): lax.all_gather(amps, 'row', axis=0, tiled=True)]
    ppermute x0 -> x7, waiting for transfers between devices: none -> 28.3 us  [the longest x4 28.3 us: collect(): from_left = lax.ppermute(from_left, axis, right)]
    ppermute x0 -> x7, starting transfers between devices: none -> 12.3 us  [the longest x3 10.4 us: collect(): from_right = lax.ppermute(from_right, axis, left)]
    dot_general x1, matrix products: 9 us -> 4.75 us  [on_device(): jnp.dot(collect(amps, 'row', 0), masked, preferred_element_type=jnp.float32)]
  transfers between devices with their start and end apart: 2 -> 8, of which waited for: 2 -> 5; matrix products, arithmetic and copies ran while one was open for 4% -> 4% of each run, Pallas kernels for 0% -> 0%
where the time goes in v1:
time: 183 us
  waiting for transfers between devices  143 us (78%)
  between operations  13.7 us (7%)
  starting transfers between devices  12.3 us (7%)
  matrix products  9.04 us (5%)
  other arithmetic  4.55 us (2%)
    psum x1, waiting for transfers between devices, on_device(): summed = lax.psum(partial_sums, 'col')  114 us
    ppermute x4, waiting for transfers between devices, collect(): from_left = lax.ppermute(from_left, axis, right)  28.3 us
    ppermute x3, starting transfers between devices, collect(): from_right = lax.ppermute(from_right, axis, left)  10.4 us
    dot_general x1, matrix products, on_device(): jnp.dot(collect(amps, 'row', 0), masked, preferred_element_type=jnp.float32)  4.75 us
    dot_general x8, matrix products, table_lookup(): jnp.dot(high_hot, padded_table, precision=lax.Precision.HIGHEST, preferre...  4.29 us
  transfers between devices with their start and end apart: 8, of which 5 were waited for; matrix products, arithmetic and copies ran while one was open for 4% of the time, Pallas kernels for 0%

profile of v1, /device:TPU:6, one launch (start us, length us, event | category | flops | bytes accessed | tf_op | source)
XLA Modules:
  0.0 183.1 jit_solution(5939161619436612491)
XLA Ops:
  6.5 0.0 all-reduce.5.cloned.1.call-start
  6.5 1.9 %collective-permute-start = (bf16[48,4096]{1,0:T(8,128)(2,1)}, bf16[48,4096]{1,0:T(8,128)(2,1)S(1)}, u32[]{:S(2)}, u32[]{:S(2)}) collective-permute-start(bf16[48,4096]{1,0:T(8,128)(2,1)} %param.11), channel_id=1, source_target_pairs={{0,32},{32,64},{64,96},{96,128},{128,160},{160,192},{192,224},{224... | collective-permute-start | bytes 1179656 | tf_op jit(solution)/shard_map/ppermute | solution.py:16
  8.5 3.9 %collective-permute-start.1 = (bf16[48,4096]{1,0:T(8,128)(2,1)}, bf16[48,4096]{1,0:T(8,128)(2,1)S(1)}, u32[]{:S(2)}, u32[]{:S(2)}) collective-permute-start(bf16[48,4096]{1,0:T(8,128)(2,1)} %param.11), channel_id=1, source_target_pairs={{0,224},{32,0},{64,32},{96,64},{128,96},{160,128},{192,160},{224,1... | collective-permute-start | bytes 1179656 | tf_op jit(solution)/shard_map/ppermute | solution.py:21
  12.4 0.7 convert_element_type.57
  13.1 0.1 reshape.50
  13.2 0.7 add_select_fusion.2
  13.9 0.7 add_select_fusion
  14.7 0.7 add_select_fusion.5
  15.4 0.0 copy-start
  15.4 0.6 fusion.6
  16.0 0.6 fusion.7
  16.6 0.7 fusion.4
  17.3 0.7 fusion.5
  18.0 0.0 copy-start.5
  18.0 0.4 broadcast_in_dim.4
  18.4 0.0 copy-done
  18.4 3.3 %collective-permute-done = bf16[48,4096]{1,0:T(8,128)(2,1)S(1)} collective-permute-done((bf16[48,4096]{1,0:T(8,128)(2,1)}, bf16[48,4096]{1,0:T(8,128)(2,1)S(1)}, u32[]{:S(2)}, u32[]{:S(2)}) %collective-permute-start) | collective-permute-done | bytes 393248 | tf_op jit(solution)/shard_map/ppermute | solution.py:16
  21.7 0.0 collective-permute-start.2
  21.7 0.0 collective-permute-done.1
  21.7 3.2 %collective-permute-start.3 = (bf16[48,4096]{1,0:T(8,128)(2,1)S(1)}, bf16[48,4096]{1,0:T(8,128)(2,1)S(1)}, u32[]{:S(2)}, u32[]{:S(2)}) collective-permute-start(bf16[48,4096]{1,0:T(8,128)(2,1)S(1)} %collective-permute-done.1), channel_id=1, source_target_pairs={{0,224},{32,0},{64,32},{96,64},{128,96},{160,128},{192,160},{224,1... | collective-permute-start | bytes 1179656 | tf_op jit(solution)/shard_map/ppermute | solution.py:21
  25.0 8.2 %collective-permute-done.2 = bf16[48,4096]{1,0:T(8,128)(2,1)S(1)} collective-permute-done((bf16[48,4096]{1,0:T(8,128)(2,1)S(1)}, bf16[48,4096]{1,0:T(8,128)(2,1)S(1)}, u32[]{:S(2)}, u32[]{:S(2)}) %collective-permute-start.2) | collective-permute-done | bytes 393248 | tf_op jit(solution)/shard_map/ppermute | solution.py:16
  33.2 0.0 collective-permute-start.4
  33.2 0.0 collective-permute-done.3
  33.2 3.2 %collective-permute-start.5 = (bf16[48,4096]{1,0:T(8,128)(2,1)S(1)}, bf16[48,4096]{1,0:T(8,128)(2,1)S(1)}, u32[]{:S(2)}, u32[]{:S(2)}) collective-permute-start(bf16[48,4096]{1,0:T(8,128)(2,1)S(1)} %collective-permute-done.3), channel_id=1, source_target_pairs={{0,224},{32,0},{64,32},{96,64},{128,96},{160,128},{192,160},{224,1... | collective-permute-start | bytes 1179656 | tf_op jit(solution)/shard_map/ppermute | solution.py:21
  36.5 7.3 %collective-permute-done.4 = bf16[48,4096]{1,0:T(8,128)(2,1)S(1)} collective-permute-done((bf16[48,4096]{1,0:T(8,128)(2,1)S(1)}, bf16[48,4096]{1,0:T(8,128)(2,1)S(1)}, u32[]{:S(2)}, u32[]{:S(2)}) %collective-permute-start.4) | collective-permute-done | bytes 393248 | tf_op jit(solution)/shard_map/ppermute | solution.py:16
  43.8 0.0 collective-permute-start.6
  43.9 0.0 collective-permute-done.5
  43.9 9.6 %collective-permute-done.6 = bf16[48,4096]{1,0:T(8,128)(2,1)S(1)} collective-permute-done((bf16[48,4096]{1,0:T(8,128)(2,1)S(1)}, bf16[48,4096]{1,0:T(8,128)(2,1)S(1)}, u32[]{:S(2)}, u32[]{:S(2)}) %collective-permute-start.6) | collective-permute-done | bytes 393248 | tf_op jit(solution)/shard_map/ppermute | solution.py:16
  53.5 0.0 copy-done.5
  53.5 0.0 copy-start.1
  53.5 0.0 copy-start.2
  53.6 0.0 copy-start.3
  53.6 0.0 copy-start.4
  53.6 4.8 %fusion = f32[384,1024]{1,0:T(8,128)} fusion(bf16[384,4096]{1,0:T(8,128)(2,1)S(1)} %constant_dynamic-update-slice_fusion, bf16[4096,1024]{1,0:T(8,128)(2,1)S(1)} %copy-done.5, s32[1024]{0:T(1024)S(1)} %convert_xor_fusion.1, s32[4096]{0:T(1024)S(1)} %convert_xor_fusion), kind=kOutput, calls=%fused_computation.1 | convolution fusion | flops 3229614080 | bytes 13127680 | tf_op jit(solution)/shard_map/dot_general | solution.py:69
  58.3 0.0 all-reduce.5.cloned.1.call-update
  58.4 0.0 copy-done.1
  58.4 0.1 reshape.51
  58.5 0.0 copy-done.2
  58.5 0.1 reshape.52
  58.5 0.6 fusion.8
  59.1 0.6 fusion.9
  59.7 0.0 copy-done.3
  59.7 0.0 copy-done.4
  59.8 0.3 fusion.10
  60.1 0.3 fusion.11
  60.4 114.2 %all-reduce.5.cloned.1.call-done = f32[384,1024]{1,0:T(8,128)} async-done(((f32[384,1024]{1,0:T(8,128)}), f32[384,1024]{1,0:T(8,128)}) %all-reduce.5.cloned.1.call-update) | async-done | bytes 1572880 | tf_op jit(solution)/shard_map/psum | solution.py:71
  174.6 1.6 subtract_divide_fusion
  (16 shorter events, 0.3 us)
Async XLA Ops:
  6.5 168.1 %all-reduce.5.cloned.1.call-start = ((), (), s32[]{:S(2)}) async-start(), calls=%async_computation | async-start | bytes 3145728 | tf_op jit(solution)/shard_map/psum | solution.py:71
  6.5 15.2 %collective-permute-start = (bf16[48,4096]{1,0:T(8,128)(2,1)}, bf16[48,4096]{1,0:T(8,128)(2,1)S(1)}, u32[]{:S(2)}, u32[]{:S(2)}) collective-permute-start(bf16[48,4096]{1,0:T(8,128)(2,1)} %param.11), channel_id=1, source_target_pairs={{0,32},{32,64},{64,96},{96,128},{128,160},{160,192},{192,224},{224... | collective-permute-start | bytes 1179656 | tf_op jit(solution)/shard_map/ppermute | solution.py:16
  8.5 13.3 %collective-permute-start.1 = (bf16[48,4096]{1,0:T(8,128)(2,1)}, bf16[48,4096]{1,0:T(8,128)(2,1)S(1)}, u32[]{:S(2)}, u32[]{:S(2)}) collective-permute-start(bf16[48,4096]{1,0:T(8,128)(2,1)} %param.11), channel_id=1, source_target_pairs={{0,224},{32,0},{64,32},{96,64},{128,96},{160,128},{192,160},{224,1... | collective-permute-start | bytes 1179656 | tf_op jit(solution)/shard_map/ppermute | solution.py:21
  15.4 3.0 %copy-start = (bf16[48,4096]{1,0:T(8,128)(2,1)S(1)}, bf16[48,4096]{1,0:T(8,128)(2,1)}, u32[]{:S(2)}) copy-start(bf16[48,4096]{1,0:T(8,128)(2,1)} %param.11) | copy-start | bytes 1179652
  18.0 35.5 %copy-start.5 = (bf16[4096,1024]{1,0:T(8,128)(2,1)S(1)}, bf16[4096,1024]{1,0:T(8,128)(2,1)}, u32[]{:S(2)}) copy-start(bf16[4096,1024]{1,0:T(8,128)(2,1)} %param.12) | copy-start | bytes 25165828
  21.7 11.5 %collective-permute-start.2 = (bf16[48,4096]{1,0:T(8,128)(2,1)S(1)}, bf16[48,4096]{1,0:T(8,128)(2,1)S(1)}, u32[]{:S(2)}, u32[]{:S(2)}) collective-permute-start(bf16[48,4096]{1,0:T(8,128)(2,1)S(1)} %collective-permute-done), channel_id=1, source_target_pairs={{0,32},{32,64},{64,96},{96,128},{128,160},{160,192},{192,224},{224... | collective-permute-start | bytes 1179656 | tf_op jit(solution)/shard_map/ppermute | solution.py:16
  21.7 11.5 %collective-permute-start.3 = (bf16[48,4096]{1,0:T(8,128)(2,1)S(1)}, bf16[48,4096]{1,0:T(8,128)(2,1)S(1)}, u32[]{:S(2)}, u32[]{:S(2)}) collective-permute-start(bf16[48,4096]{1,0:T(8,128)(2,1)S(1)} %collective-permute-done.1), channel_id=1, source_target_pairs={{0,224},{32,0},{64,32},{96,64},{128,96},{160,128},{192,160},{224,1... | collective-permute-start | bytes 1179656 | tf_op jit(solution)/shard_map/ppermute | solution.py:21
  33.2 10.6 %collective-permute-start.4 = (bf16[48,4096]{1,0:T(8,128)(2,1)S(1)}, bf16[48,4096]{1,0:T(8,128)(2,1)S(1)}, u32[]{:S(2)}, u32[]{:S(2)}) collective-permute-start(bf16[48,4096]{1,0:T(8,128)(2,1)S(1)} %collective-permute-done.2), channel_id=1, source_target_pairs={{0,32},{32,64},{64,96},{96,128},{128,160},{160,192},{192,224},{224... | collective-permute-start | bytes 1179656 | tf_op jit(solution)/shard_map/ppermute | solution.py:16
  33.2 10.6 %collective-permute-start.5 = (bf16[48,4096]{1,0:T(8,128)(2,1)S(1)}, bf16[48,4096]{1,0:T(8,128)(2,1)S(1)}, u32[]{:S(2)}, u32[]{:S(2)}) collective-permute-start(bf16[48,4096]{1,0:T(8,128)(2,1)S(1)} %collective-permute-done.3), channel_id=1, source_target_pairs={{0,224},{32,0},{64,32},{96,64},{128,96},{160,128},{192,160},{224,1... | collective-permute-start | bytes 1179656 | tf_op jit(solution)/shard_map/ppermute | solution.py:21
  43.8 9.7 %collective-permute-start.6 = (bf16[48,4096]{1,0:T(8,128)(2,1)S(1)}, bf16[48,4096]{1,0:T(8,128)(2,1)S(1)}, u32[]{:S(2)}, u32[]{:S(2)}) collective-permute-start(bf16[48,4096]{1,0:T(8,128)(2,1)S(1)} %collective-permute-done.4), channel_id=1, source_target_pairs={{0,32},{32,64},{64,96},{96,128},{128,160},{160,192},{192,224},{224... | collective-permute-start | bytes 1179656 | tf_op jit(solution)/shard_map/ppermute | solution.py:16
  53.5 4.8 %copy-start.1 = (f32[2400]{0:T(1024)S(1)}, f32[2400]{0:T(1024)}, u32[]{:S(2)}) copy-start(f32[2400]{0:T(1024)} %param.21) | copy-start | bytes 28804
  53.5 4.9 %copy-start.2 = (f32[200]{0:T(256)S(1)}, f32[200]{0:T(256)}, u32[]{:S(2)}) copy-start(f32[200]{0:T(256)} %param.20) | copy-start | bytes 2404
  53.6 6.2 %copy-start.3 = (s32[12]{0:T(128)S(1)}, s32[12]{0:T(128)}, u32[]{:S(2)}) copy-start(s32[12]{0:T(128)} %param.18) | copy-start | bytes 148
  53.6 6.2 %copy-start.4 = (s32[12]{0:T(128)S(1)}, s32[12]{0:T(128)}, u32[]{:S(2)}) copy-start(s32[12]{0:T(128)} %param.17) | copy-start | bytes 148
Sparse Core Ops, SparseCore 0:
  58.5 116.0 all-reduce.4
